TPU v7x, 128 devices: a whole 4x4x4 slice. The times are simulated.
128 devices in a mesh: ctx: 16 (over y, x), exp: 8 (over z, core).
Axes of the slice: x: 4, y: 4, z: 4, core: 2. Of those that a mesh axis runs over, the one named last changes fastest.
Arguments:
- queries: bfloat16 [4, 1024, 8192], P(None, 'ctx', 'exp'), may hold values from -2 to 2
- keys: bfloat16 [4, 1024, 8192], P(None, 'ctx', 'exp'), may hold values from -2 to 2
- values: bfloat16 [4, 1024, 8192], P(None, 'ctx', 'exp'), may hold values from -6 to 6
- decay_log: float32 [1024, 64], P('ctx', 'exp'), may hold values from -0.9 to 0
- out_gate: bfloat16 [4, 1024, 8192], P(None, 'ctx', 'exp'), may hold values from -6 to 6
- head_gain: float32 [8192], P('exp'), may hold values from 0.1 to 1.9
- out_weight: bfloat16 [8192, 6144], P('exp', 'ctx'), may hold values from -0.0625 to 0.0625
- stream: bfloat16 [4, 1024, 6144], P(None, ('ctx', 'exp')), may hold values from -6 to 6
- norm_gain: float32 [6144], replicated, may hold values from 0.1 to 1.9
- expert_ids: int32 [128, 32, 2], P(('ctx', 'exp')), may hold values from 0 to 7, all different within a row; in each aligned block of 32 rows (0 to 31, 32 to 63, ..., all dimensions but the last counted through in order) at most 9 rows name the same one
- expert_share: float32 [128, 32, 2], P(('ctx', 'exp')), may hold values from 0.2 to 1
- w_gate: bfloat16 [8, 6144, 9216], P('exp', None, 'ctx'), may hold values from -0.078125 to 0.078125
- w_up: bfloat16 [8, 6144, 9216], P('exp', None, 'ctx'), may hold values from -0.078125 to 0.078125
- w_down: bfloat16 [8, 9216, 6144], P('exp', 'ctx'), may hold values from -0.0625 to 0.0625
Outputs:
- layer_out: bfloat16 [4, 1024, 6144], P(None, ('ctx', 'exp'))
Inputs may be any that keep to these rules, and one draw needn't show every extreme that they name: `expert_ids`: within a routing group no expert takes more than 9 copies, some group gives one expert exactly 9, and the two picks of a token differ.
All inputs are finite; a program needn't handle non-finite values.
Results may differ from a plain program's by a relative error of at most 0.02.
Values may be sent and summed in bfloat16 or wider, within the bound.
A program may use at most 192 MiB of HBM per device.

v0:
```python
import jax
import jax.numpy as jnp
from jax import lax
from jax.sharding import PartitionSpec as P


def carried_in(x, axis, join, neutral):
    place = lax.axis_index(axis)
    gathered = jax.tree.map(
        lambda a, kind: lax.all_gather(a.astype(kind), axis), x, (jnp.bfloat16, jnp.bfloat16)
    )
    state = jax.tree.map(lambda a, e: jnp.zeros_like(a) + jnp.asarray(e, a.dtype), x, neutral)

    def one(lap, state):
        return join(
            state,
            jax.tree.map(
                lambda a, own: lax.dynamic_index_in_dim(a, lap, 0, False).astype(own.dtype),
                gathered,
                x,
            ),
        )

    return lax.fori_loop(0, place, one, state)


def join_states(earlier, later):
    earlier_fade, earlier_state = earlier
    later_fade, later_state = later
    return (earlier_fade * later_fade, later_fade * earlier_state + later_state)


def body(
    queries,
    keys,
    values,
    decay_log,
    out_gate,
    head_gain,
    out_weight,
    stream,
    norm_gain,
    expert_ids,
    expert_share,
    w_gate,
    w_up,
    w_down,
):
    seq_count, block_len, head_width = queries.shape
    head_count = decay_log.shape[1]
    head_dim = head_width // head_count
    split_shape = (seq_count, block_len, head_count, head_dim)
    query_heads = queries.reshape(split_shape)
    key_heads = keys.reshape(split_shape)
    value_heads = values.reshape(split_shape)
    cumulative = jnp.cumsum(decay_log, axis=0)
    position = jnp.arange(block_len)
    causal = position[:, None] >= position[None, :]
    gap_log = cumulative[:, None, :] - cumulative[None, :, :]
    decay_grid = jnp.exp(jnp.where(causal[:, :, None], gap_log, -1e30))
    scores = jnp.einsum(
        "sihd,sjhd->sijh", query_heads, key_heads, preferred_element_type=jnp.float32
    )
    weights = (scores * decay_grid[None]).astype(jnp.bfloat16)
    within = jnp.einsum("sijh,sjhd->sihd", weights, value_heads, preferred_element_type=jnp.float32)
    block_end = cumulative[-1]
    keys_faded = jnp.exp(block_end[None, :] - cumulative)[None, :, :, None] * key_heads.astype(
        jnp.float32
    )
    local_state = jnp.einsum(
        "sjhd,sjhe->shde",
        keys_faded,
        value_heads.astype(jnp.float32),
        precision=lax.Precision.HIGHEST,
    )
    fading = jnp.broadcast_to(
        jnp.exp(block_end)[None, :, None, None], (seq_count, head_count, 1, 1)
    )
    identity = (jnp.ones_like(fading), jnp.zeros_like(local_state))
    incoming_fade, incoming = carried_in((fading, local_state), "ctx", join_states, identity)
    carried = jnp.exp(cumulative)[None, :, :, None] * jnp.einsum(
        "sihd,shde->sihe",
        query_heads.astype(jnp.float32),
        incoming,
        precision=lax.Precision.HIGHEST,
    )
    attended = within + carried
    mean_square = jnp.mean(attended * attended, axis=-1, keepdims=True)
    gate_act = jax.nn.sigmoid(out_gate.reshape(split_shape).astype(jnp.float32))
    gated = (
        attended
        * lax.rsqrt(mean_square + 1e-06)
        * head_gain.reshape(head_count, head_dim)
        * gate_act
    )
    mixed = gated.astype(jnp.bfloat16).reshape(seq_count, block_len, head_width)
    sub_len = stream.shape[1]
    model_width = stream.shape[2]
    exp_count = lax.axis_size("exp")
    tok_count = seq_count * sub_len
    ordered = (
        mixed.reshape(seq_count, exp_count, sub_len, head_width)
        .transpose(1, 0, 2, 3)
        .reshape(exp_count * tok_count, head_width)
    )
    full_weight = lax.all_gather(out_weight, "ctx", axis=1, tiled=True)
    chosen_rows = ordered
    projected = lax.psum_scatter(
        jnp.dot(chosen_rows, full_weight, preferred_element_type=jnp.float32).astype(jnp.bfloat16),
        "exp",
        scatter_dimension=0,
        tiled=True,
    ).astype(jnp.float32)
    residual_sum = stream.reshape(tok_count, model_width).astype(jnp.float32) + projected
    stream_square = jnp.mean(residual_sum * residual_sum, axis=-1, keepdims=True)
    normed = (residual_sum * lax.rsqrt(stream_square + 1e-06) * norm_gain).astype(jnp.bfloat16)
    expert_local = w_gate.shape[0]
    expert_count = expert_local * exp_count
    capacity = max(2, (2 * tok_count + expert_count - 1) // expert_count + 1)
    slot_total = expert_count * capacity
    picks = expert_ids.reshape(2 * tok_count)
    one_hot = (picks[:, None] == jnp.arange(expert_count, dtype=jnp.int32)[None, :]).astype(
        jnp.int32
    )
    ranking = jnp.sum(jnp.cumsum(one_hot, axis=0) * one_hot, axis=1) - 1
    slot_of = picks * capacity + ranking
    placing = slot_of[:, None] == jnp.arange(slot_total, dtype=jnp.int32)[None, :]
    copies = jnp.repeat(normed, 2, axis=0)
    dispatch = jnp.dot(
        placing.T.astype(jnp.bfloat16), copies, preferred_element_type=jnp.float32
    ).astype(jnp.bfloat16)
    dispatch = dispatch.reshape(exp_count, expert_local, capacity, model_width)
    received = lax.all_to_all(dispatch, "exp", split_axis=0, concat_axis=0, tiled=True)
    piece = lax.all_gather(received, "ctx", axis=0, tiled=True)
    gate_part = jnp.einsum("nemd,edh->nemh", piece, w_gate, preferred_element_type=jnp.float32)
    up_part = jnp.einsum("nemd,edh->nemh", piece, w_up, preferred_element_type=jnp.float32)
    hidden_units = (jax.nn.silu(gate_part) * up_part).astype(jnp.bfloat16)
    chosen_rows = hidden_units
    summed = lax.psum_scatter(
        jnp.einsum(
            "nemh,ehd->nemd", chosen_rows, w_down, preferred_element_type=jnp.float32
        ).astype(jnp.bfloat16),
        "ctx",
        scatter_dimension=0,
        tiled=True,
    )
    returned = lax.all_to_all(summed, "exp", split_axis=0, concat_axis=0, tiled=True).reshape(
        slot_total, model_width
    )
    weighting = jnp.where(placing, expert_share.reshape(2 * tok_count, 1), 0.0)
    weighting = jnp.sum(weighting.reshape(tok_count, 2, slot_total), axis=1)
    expert_mix = jnp.dot(weighting, returned.astype(jnp.float32), precision=lax.Precision.HIGHEST)
    result = (residual_sum + expert_mix).astype(jnp.bfloat16)
    return result.reshape(seq_count, sub_len, model_width)


def solution(mesh):
    return jax.shard_map(
        body,
        mesh=mesh,
        in_specs=(
            P(None, "ctx", "exp"),
            P(None, "ctx", "exp"),
            P(None, "ctx", "exp"),
            P("ctx", "exp"),
            P(None, "ctx", "exp"),
            P("exp"),
            P("exp", "ctx"),
            P(None, ("ctx", "exp"), None),
            P(),
            P(("ctx", "exp"), None, None),
            P(("ctx", "exp"), None, None),
            P("exp", None, "ctx"),
            P("exp", None, "ctx"),
            P("exp", "ctx", None),
        ),
        out_specs=P(None, ("ctx", "exp"), None),
        check_vma=False,
    )
```

profile of v0, /device:TPU:1, one launch (start us, length us, event | category | flops | bytes accessed | tf_op | source)
XLA Modules:
  0.0 671.2 jit_solution(6845622781889080944)
XLA Ops:
  6.5 0.0 copy-start
  6.5 0.0 all-gather.10.cloned.1.call-start
  6.5 0.8 copy.71
  7.4 0.1 reduce_window_sum.22
  7.5 0.1 copy.77
  7.6 0.0 copy-done
  7.6 4.0 convolution_convert_fusion.2
  11.6 0.0 all-gather.10.cloned.1.call-update
  11.6 0.0 all-gather.6.cloned.1.call-start
  11.7 0.7 all-gather.6.cloned.1.call-update
  12.4 0.0 reduce-scatter.3.cloned.1.call-start
  12.4 0.1 copy.72
  12.5 0.7 fusion.50
  13.9 0.2 dynamic-update-slice
  14.1 34.7 %all-reduce = bf16[128]{0:T(256)(128)(2,1)S(1)} all-reduce(bf16[128]{0:T(256)(128)(2,1)S(1)} %dynamic-update-slice), channel_id=3, replica_groups=mesh['ctx'=16,'exp'=8] {'ctx'}, use_global_device_ids=true, to_apply=%add | all-reduce | flops 128 | bytes 512
  48.8 0.1 reshape.188
  48.9 0.1 copy.76
  49.0 0.1 select_exponential_fusion
  49.2 77.1 %all-gather.10.cloned.1.call-done = bf16[64,8,128,128]{3,2,1,0:T(8,128)(2,1)} async-done(((bf16[4,8,128,128]{3,2,1,0:T(8,128)(2,1)}), bf16[64,8,128,128]{3,2,1,0:T(8,128)(2,1)}) %all-gather.10.cloned.1.call-update) | async-done | bytes 16777232 | tf_op jit(solution)/shard_map/all_gather | solution.py:10
  126.3 0.2 broadcast_in_dim.28
  126.5 0.0 copy-start.3
  126.5 3.2 fusion.24
  129.7 2.3 multiply_reduce_fusion
  132.0 0.4 fusion.26
  132.4 0.3 copy.82
  132.7 0.2 reshape_reshape.3
  133.0 93.8 %all-gather.6.cloned.1.call-done = bf16[1024,6144]{1,0:T(8,128)(2,1)} async-done(((bf16[1024,384]{1,0:T(8,128)(2,1)}), bf16[1024,6144]{1,0:T(8,128)(2,1)}) %all-gather.6.cloned.1.call-update) | async-done | bytes 12582928 | tf_op jit(solution)/shard_map/all_gather | solution.py:106
  226.8 9.4 %convolution_convert_fusion = bf16[256,6144]{1,0:T(8,128)(2,1)} fusion(bf16[256,1024]{1,0:T(8,128)(2,1)S(1)} %bitcast.180, bf16[1024,6144]{1,0:T(8,128)(2,1)} %all-gather.6.cloned.1.call-done), kind=kOutput, calls=%fused_computation.7 | convolution fusion | flops 3222798336 | bytes 16252928 | tf_op jit(solution)/shard_map/dot_general | solution.py:109
  236.2 0.0 reduce-scatter.3.cloned.1.call-update
  236.2 0.0 all-gather.8.cloned.1.call-start
  236.3 0.6 copy-done.7
  236.9 0.1 copy.84
  236.9 0.1 eq.35
  237.0 0.1 fusion.47
  237.1 0.1 reduce_window_sum.23
  237.2 0.2 select_reduce_fusion.1
  237.4 31.9 %reduce-scatter.3.cloned.1.call-done = bf16[32,6144]{1,0:T(8,128)(2,1)} async-done(((bf16[256,6144]{1,0:T(8,128)(2,1)}), bf16[32,6144]{1,0:T(8,128)(2,1)}) %reduce-scatter.3.cloned.1.call-update) | async-done | bytes 393232 | tf_op jit(solution)/shard_map/reduce_scatter | solution.py:108
  269.4 1.2 multiply_reduce_fusion.1
  270.6 1.1 multiply_convert_fusion
  271.8 0.5 broadcast_in_dim.32
  272.2 0.3 reshape.172
  272.5 0.5 convolution_convert_fusion.1
  273.0 0.4 reshape.173
  273.5 27.1 %all_to_all.10 = bf16[8,1,9,6144]{3,2,1,0:T(8,128)(2,1)S(1)} all-to-all(bf16[8,1,9,6144]{3,2,1,0:T(8,128)(2,1)S(1)} %bitcast.177), channel_id=1, replica_groups=mesh['ctx'=16,'exp'=8] {'exp'}, dimensions={0} | all-to-all | bytes 1769472 | tf_op jit(solution)/shard_map/all_to_all | solution.py:133
  300.6 1.5 copy.87
  302.1 0.0 all-gather.8.cloned.1.call-update
  302.1 0.2 all-reduce.4.cloned.1.call-start
  302.3 97.3 %all-gather.8.cloned.1.call-done = bf16[128,1,9,6144]{3,0,2,1:T(8,128)(2,1)} async-done(((bf16[8,1,9,6144]{3,0,2,1:T(8,128)(2,1)}), bf16[128,1,9,6144]{3,0,2,1:T(8,128)(2,1)}) %all-gather.8.cloned.1.call-update) | async-done | bytes 14155792 | tf_op jit(solution)/shard_map/all_gather | solution.py:134
  399.6 13.7 %fusion = f32[128,9,576]{0,2,1:T(8,128)S(1)} fusion(bf16[128,1,9,6144]{3,0,2,1:T(8,128)(2,1)} %all-gather.8.cloned.1.call-done, bf16[1,6144,576]{1,2,0:T(8,128)(2,1)} %param.28), kind=kOutput, calls=%fused_computation.2 | convolution fusion | flops 8153726976 | bytes 23887872 | tf_op jit(solution)/shard_map/nemd,edh->nemh/dot_general | solution.py:136
  413.4 0.0 slice-start.1
  413.4 12.1 %fusion.17 = bf16[128,9,576]{0,2,1:T(8,128)(2,1)S(1)} fusion(f32[128,9,576]{0,2,1:T(8,128)S(1)} %fusion, bf16[1,6144,576]{1,2,0:T(8,128)(2,1)} %param.27, bf16[128,1,9,6144]{3,0,2,1:T(8,128)(2,1)S(1)} %copy-done.10), kind=kOutput, calls=%fused_computation.23 | convolution fusion | flops 8157708288 | bytes 25214976 | tf_op jit(solution)/shard_map/nemd,edh->nemh/dot_general | solution.py:135
  425.5 14.1 %convert_bitcast_fusion = bf16[128,1,9,6144]{3,0,2,1:T(8,128)(2,1)} fusion(bf16[128,9,576]{0,2,1:T(8,128)(2,1)S(1)} %fusion.17, bf16[1,576,6144]{2,1,0:T(8,128)(2,1)S(1)} %bitcast.184), kind=kOutput, calls=%fused_computation.6 | convolution fusion | flops 8160804864 | bytes 22560768 | tf_op jit(solution)/shard_map/nemh,ehd->nemd/dot_general | solution.py:140
  439.6 0.0 all-reduce.4.cloned.1.call-update
  440.3 192.9 %all-reduce.4.cloned.1.call-done = bf16[128,1,9,6144]{3,0,2,1:T(8,128)(2,1)} async-done(((bf16[128,1,9,6144]{3,0,2,1:T(8,128)(2,1)}), bf16[128,1,9,6144]{3,0,2,1:T(8,128)(2,1)}) %all-reduce.4.cloned.1.call-update) | async-done | bytes 14155792
  633.2 1.2 constant_dynamic-slice_fusion
  634.4 0.0 copy-start.9
  634.4 1.7 copy.88
  636.1 5.1 all-to-all-start.1
  641.2 0.1 sub.41
  641.3 0.1 copy.85
  641.4 0.1 select_reduce_fusion
  641.5 20.4 %all-to-all-done.1 = bf16[8,1,9,6144]{3,2,1,0:T(8,128)(2,1)S(1)} async-done(((bf16[8,1,9,6144]{3,2,1,0:T(8,128)(2,1)}), bf16[8,1,9,6144]{3,2,1,0:T(8,128)(2,1)S(1)}, u32[]{:S(2)}, u32[]{:S(2)}) %all-to-all-start.1) | async-done | bytes 884768 | tf_op jit(solution)/shard_map/all_to_all | solution.py:147
  661.9 0.4 reshape.179
  662.4 2.3 fusion.8
  (33 shorter events, 0.2 us)
Async XLA Ops:
  6.5 1.1 copy-start
  6.5 6.0 copy-start.8
  6.5 119.7 %all-gather.10.cloned.1.call-start = ((), (), s32[]{:S(2)}) async-start(), calls=%async_computation.6 | async-start | bytes 17825792 | tf_op jit(solution)/shard_map/all_gather | solution.py:10
  11.6 215.2 %all-gather.6.cloned.1.call-start = ((), (), s32[]{:S(2)}) async-start(), calls=%async_computation.3 | async-start | bytes 13369344 | tf_op jit(solution)/shard_map/all_gather | solution.py:106
  12.4 257.0 %reduce-scatter.3.cloned.1.call-start = ((), (), s32[]{:S(2)}) async-start(), calls=%async_computation.4 | async-start | bytes 3538944 | tf_op jit(solution)/shard_map/reduce_scatter | solution.py:108
  126.5 3.2 copy-start.3
  129.7 2.3 copy-start.4
  129.7 2.3 copy-start.6
  236.2 0.7 copy-start.7
  236.2 33.2 %copy-start.2 = (bf16[4,8,6144]{2,1,0:T(8,128)(2,1)S(1)}, bf16[4,8,6144]{2,1,0:T(8,128)(2,1)}, u32[]{:S(2)}) copy-start(bf16[4,8,6144]{2,1,0:T(8,128)(2,1)} %param.23) | copy-start | bytes 1179652
  236.2 34.4 %copy-start.5 = (f32[6144]{0:T(1024)S(1)}, f32[6144]{0:T(1024)}, u32[]{:S(2)}) copy-start(f32[6144]{0:T(1024)} %param.24) | copy-start | bytes 73732
  236.2 163.4 %all-gather.8.cloned.1.call-start = ((), (), s32[]{:S(2)}) async-start(), calls=%async_computation.5 | async-start | bytes 15040512 | tf_op jit(solution)/shard_map/all_gather | solution.py:134
  302.1 331.1 %all-reduce.4.cloned.1.call-start = ((), (), s32[]{:S(2)}) async-start(), calls=%async_computation.7 | async-start | bytes 28311552
  399.6 13.7 %copy-start.10 = (bf16[128,1,9,6144]{3,0,2,1:T(8,128)(2,1)S(1)}, bf16[128,1,9,6144]{3,0,2,1:T(8,128)(2,1)}, u32[]{:S(2)}) copy-start(bf16[128,1,9,6144]{3,0,2,1:T(8,128)(2,1)} %all-gather.8.cloned.1.call-done) | copy-start | bytes 42467332
  399.6 25.9 %slice-start = ((s8[7077888]{0:T(1024)(128)(4,1)}), s8[4194304]{0:T(1024)(128)(4,1)S(1)}, s32[]{:S(2)}) async-start(s8[7077888]{0:T(1024)(128)(4,1)} %bitcast.183), calls=%async_computation.8 | async-start | bytes 8388608
  413.4 12.1 %slice-start.1 = ((s8[7077888]{0:T(1024)(128)(4,1)}), s8[2883584]{0:T(1024)(128)(4,1)S(1)}, s32[]{:S(2)}) async-start(s8[7077888]{0:T(1024)(128)(4,1)} %bitcast.183), calls=%async_computation.9 | async-start | bytes 5767168
  634.4 7.0 %copy-start.9 = (f32[1,32,2]{1,2,0:T(2,128)S(1)}, f32[1,32,2]{1,2,0:T(2,128)}, u32[]{:S(2)}) copy-start(f32[1,32,2]{1,2,0:T(2,128)} %param.26) | copy-start | bytes 772
  636.1 25.8 %all-to-all-start.1 = ((bf16[8,1,9,6144]{3,2,1,0:T(8,128)(2,1)}), bf16[8,1,9,6144]{3,2,1,0:T(8,128)(2,1)S(1)}, u32[]{:S(2)}, u32[]{:S(2)}) async-start(bf16[8,1,9,6144]{3,2,1,0:T(8,128)(2,1)} %copy.88), calls=%async_computation.2 | async-start | bytes 3145728 | tf_op jit(solution)/shard_map/all_to_all | solution.py:147
  641.2 23.4 %copy-start.1 = (bf16[4,64,1024]{2,1,0:T(8,128)(2,1)S(1)}, bf16[4,64,1024]{2,1,0:T(8,128)(2,1)}, u32[]{:S(2)}) copy-start(bf16[4,64,1024]{2,1,0:T(8,128)(2,1)} %param.18) | copy-start | bytes 1572868
Sparse Core Ops, SparseCore 0:
  11.7 114.4 all-gather.9
  128.4 98.3 all-gather.5
  236.3 32.9 reduce-scatter.2
  302.2 97.3 all-gather.7
  439.8 193.3 all-reduce.3
where the time goes:
time: 672 us; the launch traced here: 671 us
  waiting for transfers between devices  514 us (76%)
  blocking collectives  61.9 us (9%)
  matrix products  61.5 us (9%)
  between operations  14.8 us (2%)
  local copies, waits for them, and re-layouts  9.89 us (1%)
    unnamed x6, waiting for transfers between devices  194 us
    all_gather x1, waiting for transfers between devices, body(): piece = lax.all_gather(received, 'ctx', axis=0, tiled=True)  97.3 us
    all_gather x1, waiting for transfers between devices, body(): full_weight = lax.all_gather(out_weight, 'ctx', axis=1, tiled=True)  93.8 us
    all_gather x1, waiting for transfers between devices, carried_in(): lax.all_gather(a.astype(kind), axis)  77.1 us
    unnamed x1, blocking collectives  34.7 us
    reduce_scatter x1, waiting for transfers between devices, body(): lax.psum_scatter(jnp.dot(chosen_rows, full_weight, preferred_element_type...  31.9 us
    all_to_all x1, blocking collectives, body(): lax.all_to_all(dispatch, 'exp', split_axis=0, concat_axis=0, tiled=True)  27.1 us
    all_to_all x1, waiting for transfers between devices, body(): lax.all_to_all(summed, 'exp', split_axis=0, concat_axis=0, tiled=True)  20.4 us
  transfers between devices with their start and end apart: 6, of which 6 were waited for; matrix products, arithmetic and copies ran while one was open for 1% of the time, Pallas kernels for 0%

commit v1 on v0

v1 whole, which is shorter than its diff:
```python
import jax
import jax.numpy as jnp
from jax import lax
from jax.sharding import Mesh, PartitionSpec as P

CTX = ("y", "x")
EXP = ("z", "c")


def incoming_states(local_state, block_end):
    pairs = local_state.shape[0] * local_state.shape[1]
    head_count = local_state.shape[1]
    n = lax.axis_size(CTX)
    per = pairs // n
    width = local_state.shape[-1]
    chunks = local_state.reshape(n, per, width, width).astype(jnp.bfloat16)
    got = lax.all_to_all(chunks, CTX, split_axis=0, concat_axis=0, tiled=True)
    ends = lax.all_gather(block_end, CTX)
    me = lax.axis_index(CTX)
    first = lax.rem(me * per, head_count)
    fade = jnp.exp(lax.dynamic_slice_in_dim(ends, first, per, 1))[:, :, None, None]
    state = jnp.zeros(got.shape[1:], jnp.float32)
    out = []
    for b in range(n):
        out.append(state.astype(jnp.bfloat16))
        state = fade[b] * state + got[b].astype(jnp.float32)
    back = lax.all_to_all(jnp.stack(out), CTX, split_axis=0, concat_axis=0, tiled=True)
    return back.reshape(local_state.shape)


def body(
    queries,
    keys,
    values,
    decay_log,
    out_gate,
    head_gain,
    out_weight,
    stream,
    norm_gain,
    expert_ids,
    expert_share,
    w_gate,
    w_up,
    w_down,
):
    seq_count, block_len, head_width = queries.shape
    head_count = decay_log.shape[1]
    head_dim = head_width // head_count
    split_shape = (seq_count, block_len, head_count, head_dim)
    query_heads = queries.reshape(split_shape)
    key_heads = keys.reshape(split_shape)
    value_heads = values.reshape(split_shape)
    position = jnp.arange(block_len)
    causal = position[:, None] >= position[None, :]
    cumulative = jnp.sum(jnp.where(causal[:, :, None], decay_log[None], 0.0), axis=1)
    gap_log = cumulative[:, None, :] - cumulative[None, :, :]
    decay_grid = jnp.exp(jnp.where(causal[:, :, None], gap_log, -1e30))
    block_end = cumulative[-1]
    keys_faded = jnp.exp(block_end[None, :] - cumulative)[None, :, :, None] * key_heads.astype(
        jnp.float32
    )
    local_state = jnp.einsum(
        "sjhd,sjhe->shde",
        keys_faded,
        value_heads.astype(jnp.float32),
        precision=lax.Precision.HIGHEST,
    )
    incoming = incoming_states(local_state, block_end)
    row_weight = lax.all_gather(out_weight, "y", axis=1, tiled=True)
    scores = jnp.einsum(
        "sihd,sjhd->sijh", query_heads, key_heads, preferred_element_type=jnp.float32
    )
    weights = (scores * decay_grid[None]).astype(jnp.bfloat16)
    within = jnp.einsum("sijh,sjhd->sihd", weights, value_heads, preferred_element_type=jnp.float32)
    carried = jnp.exp(cumulative)[None, :, :, None] * jnp.einsum(
        "sihd,shde->sihe", query_heads, incoming, preferred_element_type=jnp.float32
    )
    attended = within + carried
    mean_square = jnp.mean(attended * attended, axis=-1, keepdims=True)
    gate_act = jax.nn.sigmoid(out_gate.reshape(split_shape).astype(jnp.float32))
    gated = (
        attended
        * lax.rsqrt(mean_square + 1e-06)
        * head_gain.reshape(head_count, head_dim)
        * gate_act
    )
    mixed = gated.astype(jnp.bfloat16).reshape(seq_count, block_len, head_width)
    sub_len = stream.shape[1]
    model_width = stream.shape[2]
    exp_count = lax.axis_size(EXP)
    x_count = lax.axis_size("x")
    y_count = lax.axis_size("y")
    ctx_count = x_count * y_count
    tok_count = seq_count * sub_len
    ordered = (
        mixed.reshape(seq_count, exp_count, sub_len, head_width)
        .transpose(1, 0, 2, 3)
        .reshape(exp_count, tok_count, head_width)
    )
    row_tokens = lax.all_gather(ordered, "x", axis=1, tiled=True)
    part_width = row_weight.shape[1]
    product = jnp.dot(
        row_tokens.reshape(exp_count * x_count * tok_count, head_width),
        row_weight,
        preferred_element_type=jnp.float32,
    ).astype(jnp.bfloat16)
    column_part = lax.psum_scatter(product, EXP, scatter_dimension=0, tiled=True)
    projected = lax.all_to_all(
        column_part.reshape(x_count, tok_count, part_width), "x", split_axis=0, concat_axis=0, tiled=True
    )
    projected = (
        projected.reshape(x_count, tok_count, y_count, part_width // y_count)
        .transpose(1, 2, 0, 3)
        .reshape(tok_count, model_width)
        .astype(jnp.float32)
    )
    residual_sum = stream.reshape(tok_count, model_width).astype(jnp.float32) + projected
    stream_square = jnp.mean(residual_sum * residual_sum, axis=-1, keepdims=True)
    normed = (residual_sum * lax.rsqrt(stream_square + 1e-06) * norm_gain).astype(jnp.bfloat16)
    expert_count = exp_count
    capacity = max(2, (2 * tok_count + expert_count - 1) // expert_count + 1)
    slot_total = expert_count * capacity
    picks = expert_ids.reshape(2 * tok_count)
    copy_no = jnp.arange(2 * tok_count)
    earlier = (copy_no[None, :] < copy_no[:, None]) & (picks[None, :] == picks[:, None])
    ranking = jnp.sum(earlier.astype(jnp.int32), axis=1)
    slot_of = picks * capacity + ranking
    placing = slot_of[:, None] == jnp.arange(slot_total, dtype=jnp.int32)[None, :]
    token_placing = jnp.any(placing.reshape(tok_count, 2, slot_total), axis=1)
    dispatch = jnp.dot(
        token_placing.T.astype(jnp.bfloat16), normed, preferred_element_type=jnp.float32
    ).astype(jnp.bfloat16)
    dispatch = dispatch.reshape(exp_count, capacity, model_width)
    received = lax.all_to_all(dispatch, EXP, split_axis=0, concat_axis=0, tiled=True)
    piece = lax.all_gather(
        received.reshape(slot_total, model_width), CTX, axis=0, tiled=True
    )
    gate_part = jnp.dot(piece, w_gate[0], preferred_element_type=jnp.float32)
    up_part = jnp.dot(piece, w_up[0], preferred_element_type=jnp.float32)
    hidden_units = (jax.nn.silu(gate_part) * up_part).astype(jnp.bfloat16)
    terms = jnp.dot(hidden_units, w_down[0], preferred_element_type=jnp.float32).astype(
        jnp.bfloat16
    )
    summed = lax.psum_scatter(terms, CTX, scatter_dimension=0, tiled=True)
    returned = lax.all_to_all(
        summed.reshape(exp_count, capacity, model_width), EXP, split_axis=0, concat_axis=0, tiled=True
    ).reshape(slot_total, model_width)
    weighting = jnp.where(placing, expert_share.reshape(2 * tok_count, 1), 0.0)
    weighting = jnp.sum(weighting.reshape(tok_count, 2, slot_total), axis=1)
    expert_mix = jnp.dot(weighting, returned.astype(jnp.float32), precision=lax.Precision.HIGHEST)
    result = (residual_sum + expert_mix).astype(jnp.bfloat16)
    return result.reshape(seq_count, sub_len, model_width)


def solution(mesh):
    n_exp = mesh.shape["exp"]
    side = round(mesh.shape["ctx"] ** 0.5)
    fine = Mesh(mesh.devices.reshape(side, side, n_exp // 2, 2), ("y", "x", "z", "c"))
    return jax.shard_map(
        body,
        mesh=fine,
        in_specs=(
            P(None, CTX, EXP),
            P(None, CTX, EXP),
            P(None, CTX, EXP),
            P(CTX, EXP),
            P(None, CTX, EXP),
            P(EXP),
            P(EXP, CTX),
            P(None, CTX + EXP, None),
            P(),
            P(CTX + EXP, None, None),
            P(CTX + EXP, None, None),
            P(EXP, None, CTX),
            P(EXP, None, CTX),
            P(EXP, CTX, None),
        ),
        out_specs=P(None, CTX + EXP, None),
        check_vma=False,
    )
```

time: 672 us -> 479 us (0.71)
  waiting for transfers between devices: 514 us -> 301 us
  starting transfers between devices: 5.44 us -> 21.1 us
  other arithmetic: 3.49 us -> 13.8 us
  blocking collectives: 61.9 us -> 54.7 us
    all_gather x3, waiting for transfers between devices: 268 us -> 130 us  [the longest x1 95.5 us: body(): lax.all_gather(received.reshape(slot_total, model_width), CTX, axis=0, ti...]
    unnamed x6, waiting for transfers between devices: 194 us -> 100 us
    unnamed x1 -> x0, blocking collectives: 34.7 us -> none
    all_gather x0 -> x1, blocking collectives: none -> 25.6 us  [incoming_states(): ends = lax.all_gather(block_end, CTX)]
    all_to_all x1 -> x4, waiting for transfers between devices: 20.4 us -> 39.9 us  [the longest x1 20.6 us: body(): lax.all_to_all(summed.reshape(exp_count, capacity, model_width), EXP, spl...]
    all_to_all x1 -> x4, starting transfers between devices: 5.1 us -> 20.8 us  [the longest x1 7.58 us: incoming_states(): got = lax.all_to_all(chunks, CTX, split_axis=0, concat_axis=0, tiled=True)]
    unnamed x1 -> x14, other arithmetic: 0.01 us -> 10 us
    reshape x3 -> x5, local copies, waits for them, and re-layouts: 1.13 us -> 9.26 us  [the longest x1 2.75 us: body(): received.reshape(slot_total, model_width)]
  transfers between devices with their start and end apart: 6 -> 9, of which waited for: 6 -> 7; matrix products, arithmetic and copies ran while one was open for 1% -> 4% of each run, Pallas kernels for 0% -> 0%
where the time goes in v1:
time: 479 us; the launch traced here: 478 us
  waiting for transfers between devices  301 us (63%)
  matrix products  60.7 us (13%)
  blocking collectives  54.7 us (11%)
  starting transfers between devices  21.1 us (4%)
  other arithmetic  13.8 us (3%)
  local copies, waits for them, and re-layouts  13.4 us (3%)
  between operations  13.4 us (3%)
    unnamed x6, waiting for transfers between devices  100 us
    all_gather x1, waiting for transfers between devices, body(): lax.all_gather(received.reshape(slot_total, model_width), CTX, axis=0, ti...  95.5 us
    all_gather x1, waiting for transfers between devices, body(): row_tokens = lax.all_gather(ordered, 'x', axis=1, tiled=True)  34 us
    reduce_scatter x1, waiting for transfers between devices, body(): lax.psum_scatter(product, EXP, scatter_dimension=0, tiled=True)  31.6 us
    all_to_all x1, blocking collectives, body(): lax.all_to_all(dispatch, EXP, split_axis=0, concat_axis=0, tiled=True)  29.1 us
    all_gather x1, blocking collectives, incoming_states(): ends = lax.all_gather(block_end, CTX)  25.6 us
    all_to_all x1, waiting for transfers between devices, body(): lax.all_to_all(summed.reshape(exp_count, capacity, model_width), EXP, spl...  20.6 us
    dot_general x1, matrix products, body(): jnp.dot(hidden_units, w_down[0], preferred_element_type=jnp.float32)  17 us
  transfers between devices with their start and end apart: 9, of which 7 were waited for; matrix products, arithmetic and copies ran while one was open for 4% of the time, Pallas kernels for 0%

profile of v1, /device:TPU:1, one launch (start us, length us, event | category | flops | bytes accessed | tf_op | source)
XLA Modules:
  0.0 478.3 jit_solution(9158843161037772115)
XLA Ops:
  6.5 0.9 select_reduce_fusion
  7.4 0.2 slice_reduce_fusion
  7.7 3.9 convolution_convert_fusion.3
  11.6 7.6 %all-to-all-start = ((bf16[16,2,128,128]{3,2,1,0:T(8,128)(2,1)}), bf16[16,2,128,128]{3,2,1,0:T(8,128)(2,1)S(1)}, u32[]{:S(2)}, u32[]{:S(2)}) async-start(bf16[16,2,128,128]{3,2,1,0:T(8,128)(2,1)} %bitcast.4), calls=%async_computation | async-start | bytes 2097152 | tf_op jit(solution)/shard_map/all_to_all | solution.py:17
  19.3 0.7 all-gather.7.cloned.1.call-update
  20.0 25.6 %all-gather = f32[16,1,8]{2,1,0:T(1,128)S(1)} all-gather(f32[1,1,8]{2,1,0:T(1,128)S(1)} %bitcast.163), channel_id=1, replica_groups=mesh['y'=4,'x'=4,'z'=4,'c'=2] {'y','x'}, dimensions={0}, use_global_device_ids=true | all-gather | bytes 544 | tf_op jit(solution)/shard_map/all_gather | solution.py:18
  45.5 0.1 dynamic-slice_exponential_fusion
  45.6 0.6 constant_dynamic-update-slice_fusion
  46.3 0.7 fusion.59
  47.0 0.7 fusion.58
  47.7 0.7 convert_dynamic-update-slice_fusion.5
  48.4 0.7 fusion.57
  49.2 0.8 convert_dynamic-update-slice_fusion.4
  49.9 0.7 fusion.56
  50.6 0.7 convert_dynamic-update-slice_fusion.3
  51.3 0.7 fusion.55
  52.0 0.7 convert_dynamic-update-slice_fusion.2
  52.8 0.7 fusion.54
  53.5 0.7 convert_dynamic-update-slice_fusion.1
  54.2 0.7 fusion.53
  54.9 0.7 convert_dynamic-update-slice_fusion
  55.6 0.7 fusion.52
  56.3 0.7 fusion.60
  57.0 3.7 all-to-all-start.1
  60.7 0.1 select_exponential_fusion
  60.9 0.1 copy.78
  61.0 13.1 %all-to-all-done.1 = bf16[16,2,128,128]{3,2,1,0:T(8,128)(2,1)S(1)} async-done(((bf16[16,2,128,128]{3,2,1,0:T(8,128)(2,1)}), bf16[16,2,128,128]{3,2,1,0:T(8,128)(2,1)S(1)}, u32[]{:S(2)}, u32[]{:S(2)}) %all-to-all-start.1) | async-done | bytes 1048608 | tf_op jit(solution)/shard_map/all_to_all | solution.py:27
  74.2 0.4 fusion.15
  74.6 1.9 multiply_reduce_fusion
  76.5 1.4 fusion.17
  77.9 0.3 copy.85
  78.2 0.2 reshape_reshape.3
  78.4 0.9 copy_bitcast_fusion.1
  79.4 34.0 %all-gather.5.cloned.1.call-done = bf16[8,128,1024]{2,1,0:T(8,128)(2,1)} async-done(((bf16[8,32,1024]{2,1,0:T(8,128)(2,1)}), bf16[8,128,1024]{2,1,0:T(8,128)(2,1)}) %all-gather.5.cloned.1.call-update) | async-done | bytes 2097168 | tf_op jit(solution)/shard_map/all_gather | solution.py:101
  113.5 7.6 %convolution_convert_fusion.2 = bf16[1024,1536]{1,0:T(8,128)(2,1)} fusion(bf16[1024,1024]{1,0:T(8,128)(2,1)} %bitcast.166, bf16[1024,1536]{1,0:T(8,128)(2,1)} %all-gather.7.cloned.1.call-done), kind=kOutput, calls=%fused_computation.11 | convolution fusion | flops 3222798336 | bytes 8388608 | tf_op jit(solution)/shard_map/dot_general | solution.py:103
  121.1 0.7 copy-done.6
  121.7 0.1 copy.88
  121.8 0.1 eq.30
  121.9 0.2 convert_reduce_fusion
  122.1 0.1 reduce_sum.50
  122.3 31.6 %reduce-scatter.5.cloned.1.call-done = bf16[128,1536]{1,0:T(8,128)(2,1)} async-done(((bf16[1024,1536]{1,0:T(8,128)(2,1)}), bf16[128,1536]{1,0:T(8,128)(2,1)}) %reduce-scatter.5.cloned.1.call-update) | async-done | bytes 393232 | tf_op jit(solution)/shard_map/reduce_scatter | solution.py:108
  153.9 4.1 all-to-all-start.2
  158.1 6.1 %all-to-all-done.2 = bf16[4,32,1536]{2,1,0:T(8,128)(2,1)S(1)} async-done(((bf16[4,32,1536]{2,1,0:T(8,128)(2,1)}), bf16[4,32,1536]{2,1,0:T(8,128)(2,1)S(1)}, u32[]{:S(2)}, u32[]{:S(2)}) %all-to-all-start.2) | async-done | bytes 393248 | tf_op jit(solution)/shard_map/all_to_all | solution.py:109
  164.3 0.2 reshape.229
  164.5 0.5 copy.130
  165.0 0.3 reshape.228
  165.4 0.3 reshape.227
  165.8 0.2 fusion.23
  166.0 0.1 rsqrt.21
  166.1 1.4 convolution_convert_fusion.1
  167.4 1.6 reshape.219
  169.0 29.1 %all_to_all.25 = bf16[8,9,6144]{2,1,0:T(8,128)(2,1)} all-to-all(bf16[8,9,6144]{2,1,0:T(8,128)(2,1)S(1)} %reshape.219), channel_id=1, replica_groups=mesh['y'=4,'x'=4,'z'=4,'c'=2] {'z','c'}, dimensions={0} | all-to-all | bytes 1769472 | tf_op jit(solution)/shard_map/all_to_all | solution.py:135
  198.2 2.8 reshape.220
  200.9 0.2 reduce-scatter.7.cloned.1.call-start
  201.2 95.5 %all-gather.9.cloned.1.call-done = bf16[1152,6144]{1,0:T(8,128)(2,1)} async-done(((bf16[72,6144]{1,0:T(8,128)(2,1)}), bf16[1152,6144]{1,0:T(8,128)(2,1)}) %all-gather.9.cloned.1.call-update) | async-done | bytes 14155792 | tf_op jit(solution)/shard_map/all_gather | solution.py:136
  296.7 13.7 %fusion.3 = f32[1152,576]{0,1:T(8,128)S(1)} fusion(bf16[1152,6144]{1,0:T(8,128)(2,1)} %all-gather.9.cloned.1.call-done, bf16[1,6144,576]{1,2,0:T(8,128)(2,1)} %param.25), kind=kOutput, calls=%fused_computation.4 | convolution fusion | flops 8153726976 | bytes 23887872 | tf_op jit(solution)/shard_map/dot_general | solution.py:139
  310.4 12.3 %fusion.10 = bf16[1152,576]{0,1:T(8,128)(2,1)S(1)} fusion(bf16[1152,6144]{1,0:T(8,128)(2,1)S(1)} %copy-done.8, bf16[1,6144,576]{1,2,0:T(8,128)(2,1)} %param.26, f32[1152,576]{0,1:T(8,128)S(1)} %fusion.3), kind=kOutput, calls=%fused_computation.12 | convolution fusion | flops 8157708288 | bytes 25214976 | tf_op jit(solution)/shard_map/dot_general | solution.py:140
  322.8 17.0 %convolution_convert_fusion = bf16[1152,6144]{1,0:T(8,128)(2,1)} fusion(bf16[1152,576]{0,1:T(8,128)(2,1)S(1)} %fusion.10, bf16[1,576,6144]{2,1,0:T(8,128)(2,1)} %param.27), kind=kOutput, calls=%fused_computation | convolution fusion | flops 8160804864 | bytes 22560768 | tf_op jit(solution)/shard_map/dot_general | solution.py:142
  339.8 99.4 %reduce-scatter.7.cloned.1.call-done = bf16[72,6144]{1,0:T(8,128)(2,1)} async-done(((bf16[1152,6144]{1,0:T(8,128)(2,1)}), bf16[72,6144]{1,0:T(8,128)(2,1)}) %reduce-scatter.7.cloned.1.call-update) | async-done | bytes 884752
  439.1 2.7 reshape.221
  441.9 5.4 %all-to-all-start.4 = ((bf16[8,9,6144]{2,1,0:T(8,128)(2,1)}), bf16[8,9,6144]{2,1,0:T(8,128)(2,1)S(1)}, u32[]{:S(2)}, u32[]{:S(2)}) async-start(bf16[8,9,6144]{2,1,0:T(8,128)(2,1)} %reshape.221), calls=%async_computation.5 | async-start | bytes 3145728 | tf_op jit(solution)/shard_map/all_to_all | solution.py:146
  447.4 20.6 %all-to-all-done.4 = bf16[8,9,6144]{2,1,0:T(8,128)(2,1)S(1)} async-done(((bf16[8,9,6144]{2,1,0:T(8,128)(2,1)}), bf16[8,9,6144]{2,1,0:T(8,128)(2,1)S(1)}, u32[]{:S(2)}, u32[]{:S(2)}) %all-to-all-start.4) | async-done | bytes 884768 | tf_op jit(solution)/shard_map/all_to_all | solution.py:146
  468.0 1.3 reshape.222
  469.3 2.5 fusion.6
  (36 shorter events, 0.6 us)
Async XLA Ops:
  6.5 1.2 copy-start
  11.6 34.7 %all-to-all-start = ((bf16[16,2,128,128]{3,2,1,0:T(8,128)(2,1)}), bf16[16,2,128,128]{3,2,1,0:T(8,128)(2,1)S(1)}, u32[]{:S(2)}, u32[]{:S(2)}) async-start(bf16[16,2,128,128]{3,2,1,0:T(8,128)(2,1)} %bitcast.4), calls=%async_computation | async-start | bytes 2097152 | tf_op jit(solution)/shard_map/all_to_all | solution.py:17
  19.2 60.2 %all-gather.7.cloned.1.call-start = ((), (), s32[]{:S(2)}) async-start(), calls=%async_computation.8 | async-start | bytes 3932160 | tf_op jit(solution)/shard_map/all_gather | solution.py:70
  49.9 24.3 %copy-start.3 = (bf16[4,64,1024]{2,1,0:T(8,128)(2,1)S(1)}, bf16[4,64,1024]{2,1,0:T(8,128)(2,1)}, u32[]{:S(2)}) copy-start(bf16[4,64,1024]{2,1,0:T(8,128)(2,1)} %param.14) | copy-start | bytes 1572868
  57.0 17.1 %all-to-all-start.1 = ((bf16[16,2,128,128]{3,2,1,0:T(8,128)(2,1)}), bf16[16,2,128,128]{3,2,1,0:T(8,128)(2,1)S(1)}, u32[]{:S(2)}, u32[]{:S(2)}) async-start(bf16[16,2,128,128]{3,2,1,0:T(8,128)(2,1)} %fusion.60), calls=%async_computation.1 | async-start | bytes 2097152 | tf_op jit(solution)/shard_map/all_to_all | solution.py:27
  60.7 52.8 %all-gather.5.cloned.1.call-start = ((), (), s32[]{:S(2)}) async-start(), calls=%async_computation.7 | async-start | bytes 2621440 | tf_op jit(solution)/shard_map/all_gather | solution.py:101
  74.2 2.3 copy-start.5
  79.3 74.6 %reduce-scatter.5.cloned.1.call-start = ((), (), s32[]{:S(2)}) async-start(), calls=%async_computation.9 | async-start | bytes 3538944 | tf_op jit(solution)/shard_map/reduce_scatter | solution.py:108
  121.0 0.7 copy-start.6
  153.9 10.3 %all-to-all-start.2 = ((bf16[4,32,1536]{2,1,0:T(8,128)(2,1)}), bf16[4,32,1536]{2,1,0:T(8,128)(2,1)S(1)}, u32[]{:S(2)}, u32[]{:S(2)}) async-start(bf16[4,32,1536]{2,1,0:T(8,128)(2,1)} %bitcast.162), calls=%async_computation.3 | async-start | bytes 786432 | tf_op jit(solution)/shard_map/all_to_all | solution.py:109
  158.0 7.7 %copy-start.2 = (bf16[4,8,6144]{2,1,0:T(8,128)(2,1)S(1)}, bf16[4,8,6144]{2,1,0:T(8,128)(2,1)}, u32[]{:S(2)}) copy-start(bf16[4,8,6144]{2,1,0:T(8,128)(2,1)} %param.21) | copy-start | bytes 1179652
  158.0 138.6 %all-gather.9.cloned.1.call-start = ((), (), s32[]{:S(2)}) async-start(), calls=%async_computation.10 | async-start | bytes 15040512 | tf_op jit(solution)/shard_map/all_gather | solution.py:136
  164.5 1.5 copy-start.4
  200.9 238.2 %reduce-scatter.7.cloned.1.call-start = ((), (), s32[]{:S(2)}) async-start(), calls=%async_computation.11 | async-start | bytes 15040512
  296.7 13.8 %copy-start.8 = (bf16[1152,6144]{1,0:T(8,128)(2,1)S(1)}, bf16[1152,6144]{1,0:T(8,128)(2,1)}, u32[]{:S(2)}) copy-start(bf16[1152,6144]{1,0:T(8,128)(2,1)} %all-gather.9.cloned.1.call-done) | copy-start | bytes 42467332
  339.8 107.5 %copy-start.7 = (f32[1,32,2]{1,2,0:T(2,128)S(1)}, f32[1,32,2]{1,2,0:T(2,128)}, u32[]{:S(2)}) copy-start(f32[1,32,2]{1,2,0:T(2,128)} %param.24) | copy-start | bytes 772
  441.9 26.1 %all-to-all-start.4 = ((bf16[8,9,6144]{2,1,0:T(8,128)(2,1)}), bf16[8,9,6144]{2,1,0:T(8,128)(2,1)S(1)}, u32[]{:S(2)}, u32[]{:S(2)}) async-start(bf16[8,9,6144]{2,1,0:T(8,128)(2,1)} %reshape.221), calls=%async_computation.5 | async-start | bytes 3145728 | tf_op jit(solution)/shard_map/all_to_all | solution.py:146
  447.3 24.5 %copy-start.1 = (bf16[4,64,1024]{2,1,0:T(8,128)(2,1)S(1)}, bf16[4,64,1024]{2,1,0:T(8,128)(2,1)}, u32[]{:S(2)}) copy-start(bf16[4,64,1024]{2,1,0:T(8,128)(2,1)} %param.16) | copy-start | bytes 1572868
Sparse Core Ops, SparseCore 0:
  21.7 42.4 all-gather.6
  79.5 33.9 all-gather.4
  121.2 32.6 reduce-scatter.4
  201.1 95.5 all-gather.8
  339.9 99.1 reduce-scatter.6
